TPU v7x, 256 devices: a whole 4x4x8 slice. The times are simulated.
256 devices in a mesh: stripe: 32 (over z, x_lo, core), tile: 8 (over y, x_hi).
Axes of the slice: x: 4 (x_hi: 2, x_lo: 2; x = x_hi * 2 + x_lo), y: 4, z: 8, core: 2. Of those that a mesh axis runs over, the one named last changes fastest.
Arguments:
- positions: int32 [32, 24], P('stripe', 'tile'), may hold values from -64 to -64, as said below
- row_offsets: int32 [32, 24], P('stripe', 'tile'), may hold values from -64 to 64, as said below
- amplitudes: float32 [32, 24, 256, 256], P('stripe', 'tile'), may hold values from 0 to 2
- object_field: float32 [2, 8192, 1024], P(None, 'stripe', 'tile'), may hold values from -6 to 6
- probe_field: float32 [2, 256, 256], replicated, may hold values from -6 to 6
Outputs:
- object_out: float32 [2, 8192, 1024], P(None, 'stripe', 'tile')
- probe_out: float32 [2, 256, 256], replicated
Inputs may be any that keep to these rules, and one draw needn't show every extreme that they name: `positions`: in every block of 3 patterns of one stripe and one tile, the first offset is -64 and the second is 128 - 192. `row_offsets`: in every block of 3 patterns of one stripe and one tile, the first row offset is -64 and the second is 64.
All inputs are finite; a program needn't handle non-finite values.
Results may differ from a plain program's by a relative error of at most 0.0006.
The roundings to bfloat16 on the way count: a program that leaves them out, or rounds other values in their place, can miss the bound.
Values sent between devices are 32-bit elements; how exact they have to be, the bound alone decides.
No kernel may reach another device: no remote copies, remote signals or barrier semaphores. Data moves between devices by JAX's collectives and lax.ppermute only.
A program may use at most 64 MiB of HBM per device.

v0:
```python
import math
import jax
import jax.numpy as jnp
from jax import lax
from jax.sharding import PartitionSpec as P

PW = 256
HALO = 64
TILE_W = 128
PAT_DEV = 3
INNER = 2
OUTER = 2


def padded(x, sides, width):
    for axis, dim in sides:
        count, length = (lax.axis_size(axis), x.shape[dim])
        up = [(i, (i + 1) % count) for i in range(count - 1)]
        down = [(j, i) for i, j in up]
        last = lax.slice_in_dim(x, length - width, length, axis=dim)
        first = lax.slice_in_dim(x, 0, width, axis=dim)
        before = lax.ppermute(last, axis, up)
        after = lax.ppermute(first, axis, down)
        x = jnp.concatenate([before, x, after], axis=dim)
    return x


def from_behind(value, axis, steps):
    count = lax.axis_size(axis)
    first, last = (max(0, -steps), min(count, count - steps))
    return lax.ppermute(value, axis, [(source, source + steps) for source in range(first, last)])


def dft_tables():
    indices = jnp.arange(PW, dtype=jnp.int32)
    phase = indices[:, None] * indices[None, :] % PW
    angles = phase.astype(jnp.float32) * (2.0 * math.pi / PW)
    factor = 1.0 / math.sqrt(PW)
    return (
        (jnp.cos(angles) * factor).astype(jnp.bfloat16),
        (jnp.sin(angles) * factor).astype(jnp.bfloat16),
    )


def apply_left(matrix, batch):
    return jnp.einsum("kn,pnm->pkm", matrix, batch, preferred_element_type=jnp.float32)


def apply_right(batch, matrix):
    return jnp.einsum("pkn,nm->pkm", batch, matrix, preferred_element_type=jnp.float32)


def pattern_pass(windows, probe_field, measured, cosine, sine):
    win_re = windows[:, 0]
    win_im = windows[:, 1]
    probe_re = probe_field[0]
    probe_im = probe_field[1]
    exit_re = (probe_re * win_re - probe_im * win_im).astype(jnp.bfloat16)
    exit_im = (probe_re * win_im + probe_im * win_re).astype(jnp.bfloat16)
    half_re = (apply_left(cosine, exit_re) + apply_left(sine, exit_im)).astype(jnp.bfloat16)
    half_im = (apply_left(cosine, exit_im) - apply_left(sine, exit_re)).astype(jnp.bfloat16)
    spec_re = apply_right(half_re, cosine) + apply_right(half_im, sine)
    spec_im = apply_right(half_im, cosine) - apply_right(half_re, sine)
    magnitude = jnp.sqrt(spec_re * spec_re + spec_im * spec_im)
    scaling = measured / jnp.maximum(magnitude, 0.5)
    miss_re = (spec_re - scaling * spec_re).astype(jnp.bfloat16)
    miss_im = (spec_im - scaling * spec_im).astype(jnp.bfloat16)
    hb_re = (apply_left(cosine, miss_re) - apply_left(sine, miss_im)).astype(jnp.bfloat16)
    hb_im = (apply_left(cosine, miss_im) + apply_left(sine, miss_re)).astype(jnp.bfloat16)
    back_re = apply_right(hb_re, cosine) - apply_right(hb_im, sine)
    back_im = apply_right(hb_im, cosine) + apply_right(hb_re, sine)
    object_grad = jnp.stack(
        [probe_re * back_re + probe_im * back_im, probe_re * back_im - probe_im * back_re], axis=1
    )
    probe_grad = jnp.stack(
        [
            jnp.sum(win_re * back_re + win_im * back_im, axis=0),
            jnp.sum(win_re * back_im - win_im * back_re, axis=0),
        ]
    )
    illumination = jnp.sum(win_re * win_re + win_im * win_im, axis=0)
    return (object_grad, probe_grad, illumination)


def per_device(positions, row_offsets, amplitudes, object_field, probe_field):
    cosine, sine = dft_tables()
    column_starts = positions[0] + HALO
    row_starts = row_offsets[0] + HALO
    measured = amplitudes[0]
    rows_ext = PW + 2 * HALO
    columns_ext = TILE_W + 2 * HALO
    zero_index = jnp.zeros((), jnp.int32)
    current = object_field
    extended = object_field
    for outer_step in range(OUTER):
        grad_sum = jnp.zeros((2, PW, PW), jnp.float32)
        light_sum = jnp.zeros((PW, PW), jnp.float32)
        step_size = 1.0 / (
            2.0
            * PAT_DEV
            * jnp.max(probe_field[0] * probe_field[0] + probe_field[1] * probe_field[1])
            + 1e-06
        )
        for inner_step in range(INNER):
            extended = padded(current, (("stripe", 1), ("tile", 2)), HALO)
            windows = jax.vmap(
                lambda row_start, column_start: lax.dynamic_slice(
                    extended, (zero_index, row_start, column_start), (2, PW, PW)
                )
            )(row_starts, column_starts)
            object_grad, grad_sum, light_sum = pattern_pass(
                windows, probe_field, measured, cosine, sine
            )
            gradient = jnp.zeros((2, rows_ext, columns_ext), jnp.float32)
            for pattern in range(PAT_DEV):
                where = (zero_index, row_starts[pattern], column_starts[pattern])
                before = lax.dynamic_slice(gradient, where, (2, PW, PW))
                gradient = lax.dynamic_update_slice(gradient, before + object_grad[pattern], where)
            from_left = from_behind(gradient[:, :, HALO + TILE_W :], "tile", 1)
            from_right = from_behind(gradient[:, :, :HALO], "tile", -1)
            middle = gradient[:, :, HALO : HALO + TILE_W]
            middle = middle.at[:, :, :HALO].add(from_left)
            middle = middle.at[:, :, TILE_W - HALO :].add(from_right)
            from_above = from_behind(middle[:, HALO + PW :, :], "stripe", 1)
            from_below = from_behind(middle[:, :HALO, :], "stripe", -1)
            own_grad = middle[:, HALO : HALO + PW, :]
            own_grad = own_grad.at[:, :HALO, :].add(from_above)
            own_grad = own_grad.at[:, PW - HALO :, :].add(from_below)
            current = current - step_size * own_grad
        total_grad, total_light = lax.psum((grad_sum, light_sum), ("stripe", "tile"))
        probe_field = probe_field - 0.5 * total_grad / (total_light + 1.0)
    return (current, probe_field)


def solution(mesh):
    placed = (
        P("stripe", "tile"),
        P("stripe", "tile"),
        P("stripe", "tile", None, None),
        P(None, "stripe", "tile"),
        P(),
    )
    return jax.shard_map(
        per_device,
        mesh=mesh,
        in_specs=placed,
        out_specs=(P(None, "stripe", "tile"), P()),
        check_vma=False,
    )
```

profile of v0, /device:TPU:2, one launch (start us, length us, event | category | flops | bytes accessed | tf_op | source)
XLA Modules:
  0.0 924.7 jit_solution(10686164837930913628)
XLA Ops:
  21.8 4.1 collective-permute-start.2
  27.2 7.7 collective-permute-done.2
  35.0 11.0 %collective-permute-done.3 = f32[2,384,64]{2,0,1:T(2,128)S(1)} collective-permute-done((f32[2,384,64]{2,0,1:T(2,128)S(1)}, f32[2,384,64]{2,0,1:T(2,128)S(1)}, u32[]{:S(2)}, u32[]{:S(2)}) %collective-permute-start.3) | collective-permute-done | bytes 196640 | tf_op jit(solution)/shard_map/ppermute | solution.py:23
  70.4 12.6 %subtract_bitcast_fusion.3 = (f32[3,1,256,256]{3,2,0,1:T(8,128)S(1)}, f32[3,1,256,256]{3,2,0,1:T(8,128)S(1)}) fusion(f32[3,256,256]{2,1,0:T(8,128)S(1)} %convolution_add_fusion.12, f32[256,256]{1,0:T(8,128)S(1)} %get-tuple-element.251, f32[256,256]{1,0:T(8,128)S(1)} %get-tuple-element.250, f32[3,256,256]{2,1,0:T(8,128)S(1)} %fusion.160, ...), kind=kOutput, calls=%fused_computation.134 | convolution fusion | flops 103088128 | bytes 4063232 | tf_op jit(solution)/shard_map/pkn,nm->pkm/dot_general | solution.py:50
  90.8 4.5 collective-permute-start.4
  96.7 7.2 collective-permute-done.4
  105.1 9.0 collective-permute-done.5
  132.5 5.2 collective-permute-start.10
  139.0 7.8 collective-permute-done.10
  146.8 9.7 %collective-permute-done.11 = f32[2,384,64]{2,1,0:T(8,128)S(1)} collective-permute-done((f32[2,384,64]{2,1,0:T(8,128)S(1)}, f32[2,384,64]{2,1,0:T(8,128)S(1)}, u32[]{:S(2)}, u32[]{:S(2)}) %collective-permute-start.11) | collective-permute-done | bytes 196640 | tf_op jit(solution)/shard_map/ppermute | solution.py:23
  191.4 5.3 collective-permute-start.12
  198.2 8.0 collective-permute-done.12
  207.2 8.2 collective-permute-done.13
  224.7 5.0 collective-permute-start.16
  236.4 251.6 %all-reduce.7.cloned.1.call-done = (f32[2,256,256]{2,1,0:T(8,128)}, f32[256,256]{1,0:T(8,128)}) async-done(((f32[2,256,256]{2,1,0:T(8,128)}, f32[256,256]{1,0:T(8,128)}), (f32[2,256,256]{2,1,0:T(8,128)}, f32[256,256]{1,0:T(8,128)})) %all-reduce.7.cloned.1.call-update) | async-done | bytes 786448 | tf_op jit(solution)/shard_map/psum | solution.py:130
  536.9 5.4 collective-permute-done.20
  543.3 10.0 %collective-permute-done.21 = f32[2,384,64]{2,1,0:T(8,128)S(1)} collective-permute-done((f32[2,384,64]{2,1,0:T(8,128)S(1)}, f32[2,384,64]{2,1,0:T(8,128)S(1)}, u32[]{:S(2)}, u32[]{:S(2)}) %collective-permute-start.21) | collective-permute-done | bytes 196640 | tf_op jit(solution)/shard_map/ppermute | solution.py:31
  564.1 4.6 collective-permute-start.24
  577.2 7.7 collective-permute-done.26
  584.9 10.9 %collective-permute-done.27 = f32[2,384,64]{2,1,0:T(8,128)S(1)} collective-permute-done((f32[2,384,64]{2,1,0:T(8,128)S(1)}, f32[2,384,64]{2,1,0:T(8,128)S(1)}, u32[]{:S(2)}, u32[]{:S(2)}) %collective-permute-start.27) | collective-permute-done | bytes 196640 | tf_op jit(solution)/shard_map/ppermute | solution.py:23
  630.7 4.2 collective-permute-start.28
  636.3 7.9 collective-permute-done.28
  645.3 10.4 %collective-permute-done.29 = f32[2,384,64]{2,1,0:T(8,128)S(1)} collective-permute-done((f32[2,384,64]{2,1,0:T(8,128)S(1)}, f32[2,384,64]{2,1,0:T(8,128)S(1)}, u32[]{:S(2)}, u32[]{:S(2)}) %collective-permute-start.29) | collective-permute-done | bytes 196640 | tf_op jit(solution)/shard_map/ppermute | solution.py:31
  666.7 247.8 %all-reduce.5.cloned.1.call-done = (f32[2,256,256]{2,1,0:T(8,128)}, f32[256,256]{1,0:T(8,128)}) async-done(((f32[2,256,256]{2,1,0:T(8,128)}, f32[256,256]{1,0:T(8,128)}), (f32[2,256,256]{2,1,0:T(8,128)}, f32[256,256]{1,0:T(8,128)})) %all-reduce.5.cloned.1.call-update) | async-done | bytes 786448 | tf_op jit(solution)/shard_map/psum | solution.py:130
  (264 shorter events, 236.0 us)
Async XLA Ops:
  7.2 480.8 %all-reduce.7.cloned.1.call-start = ((), (), s32[]{:S(2)}) async-start(), calls=%async_computation.1 | async-start | bytes 1572864 | tf_op jit(solution)/shard_map/psum | solution.py:130
  8.2 12.9 %collective-permute-start = (f32[2,64,128]{2,0,1:T(2,128)S(1)}, f32[2,64,128]{2,0,1:T(2,128)S(1)}, u32[]{:S(2)}, u32[]{:S(2)}) collective-permute-start(f32[2,64,128]{2,0,1:T(2,128)S(1)} %copy.230), channel_id=1, source_target_pairs={{0,8},{8,16},{16,24},{24,32},{32,40},{40,48},{48,56},{56,64},{64,7... | collective-permute-start | bytes 196616 | tf_op jit(solution)/shard_map/ppermute | solution.py:22
  10.2 11.2 %collective-permute-start.1 = (f32[2,64,128]{2,0,1:T(2,128)S(1)}, f32[2,64,128]{2,0,1:T(2,128)S(1)}, u32[]{:S(2)}, u32[]{:S(2)}) collective-permute-start(f32[2,64,128]{2,0,1:T(2,128)S(1)} %copy.231), channel_id=1, source_target_pairs={{8,0},{16,8},{24,16},{32,24},{40,32},{48,40},{56,48},{64,56},{72,6... | collective-permute-start | bytes 196616 | tf_op jit(solution)/shard_map/ppermute | solution.py:23
  21.8 13.1 %collective-permute-start.2 = (f32[2,384,64]{2,0,1:T(2,128)S(1)}, f32[2,384,64]{2,0,1:T(2,128)S(1)}, u32[]{:S(2)}, u32[]{:S(2)}) collective-permute-start(f32[2,384,64]{2,0,1:T(2,128)S(1)} %get-tuple-element.266), channel_id=1, source_target_pairs={{0,1},{1,2},{2,3},{3,4},{4,5},{5,6},{6,7},{8,9},{9,10},{10,11},{11... | collective-permute-start | bytes 589832 | tf_op jit(solution)/shard_map/ppermute | solution.py:22
  25.9 20.1 %collective-permute-start.3 = (f32[2,384,64]{2,0,1:T(2,128)S(1)}, f32[2,384,64]{2,0,1:T(2,128)S(1)}, u32[]{:S(2)}, u32[]{:S(2)}) collective-permute-start(f32[2,384,64]{2,0,1:T(2,128)S(1)} %get-tuple-element.267), channel_id=1, source_target_pairs={{1,0},{2,1},{3,2},{4,3},{5,4},{6,5},{7,6},{9,8},{10,9},{11,10},{12... | collective-permute-start | bytes 589832 | tf_op jit(solution)/shard_map/ppermute | solution.py:23
  90.8 13.2 %collective-permute-start.4 = (f32[2,384,64]{2,1,0:T(8,128)S(1)}, f32[2,384,64]{2,1,0:T(8,128)S(1)}, u32[]{:S(2)}, u32[]{:S(2)}) collective-permute-start(f32[2,384,64]{2,1,0:T(8,128)S(1)} %get-tuple-element.247), channel_id=1, source_target_pairs={{0,1},{1,2},{2,3},{3,4},{4,5},{5,6},{6,7},{8,9},{9,10},{10,11},{11... | collective-permute-start | bytes 589832 | tf_op jit(solution)/shard_map/ppermute | solution.py:31
  95.4 18.7 %collective-permute-start.5 = (f32[2,384,64]{2,1,0:T(8,128)S(1)}, f32[2,384,64]{2,1,0:T(8,128)S(1)}, u32[]{:S(2)}, u32[]{:S(2)}) collective-permute-start(f32[2,384,64]{2,1,0:T(8,128)S(1)} %get-tuple-element.246), channel_id=1, source_target_pairs={{1,0},{2,1},{3,2},{4,3},{5,4},{6,5},{7,6},{9,8},{10,9},{11,10},{12... | collective-permute-start | bytes 589832 | tf_op jit(solution)/shard_map/ppermute | solution.py:31
  115.9 7.0 collective-permute-start.6
  132.5 14.3 %collective-permute-start.10 = (f32[2,384,64]{2,1,0:T(8,128)S(1)}, f32[2,384,64]{2,1,0:T(8,128)S(1)}, u32[]{:S(2)}, u32[]{:S(2)}) collective-permute-start(f32[2,384,64]{2,1,0:T(8,128)S(1)} %get-tuple-element.262), channel_id=1, source_target_pairs={{0,1},{1,2},{2,3},{3,4},{4,5},{5,6},{6,7},{8,9},{9,10},{10,11},{11... | collective-permute-start | bytes 589832 | tf_op jit(solution)/shard_map/ppermute | solution.py:22
  137.7 18.8 %collective-permute-start.11 = (f32[2,384,64]{2,1,0:T(8,128)S(1)}, f32[2,384,64]{2,1,0:T(8,128)S(1)}, u32[]{:S(2)}, u32[]{:S(2)}) collective-permute-start(f32[2,384,64]{2,1,0:T(8,128)S(1)} %get-tuple-element.263), channel_id=1, source_target_pairs={{1,0},{2,1},{3,2},{4,3},{5,4},{6,5},{7,6},{9,8},{10,9},{11,10},{12... | collective-permute-start | bytes 589832 | tf_op jit(solution)/shard_map/ppermute | solution.py:23
  191.4 14.8 %collective-permute-start.12 = (f32[2,384,64]{2,1,0:T(8,128)S(1)}, f32[2,384,64]{2,1,0:T(8,128)S(1)}, u32[]{:S(2)}, u32[]{:S(2)}) collective-permute-start(f32[2,384,64]{2,1,0:T(8,128)S(1)} %get-tuple-element.245), channel_id=1, source_target_pairs={{0,1},{1,2},{2,3},{3,4},{4,5},{5,6},{6,7},{8,9},{9,10},{10,11},{11... | collective-permute-start | bytes 589832 | tf_op jit(solution)/shard_map/ppermute | solution.py:31
  196.9 18.5 %collective-permute-start.13 = (f32[2,384,64]{2,1,0:T(8,128)S(1)}, f32[2,384,64]{2,1,0:T(8,128)S(1)}, u32[]{:S(2)}, u32[]{:S(2)}) collective-permute-start(f32[2,384,64]{2,1,0:T(8,128)S(1)} %get-tuple-element.244), channel_id=1, source_target_pairs={{1,0},{2,1},{3,2},{4,3},{5,4},{6,5},{7,6},{9,8},{10,9},{11,10},{12... | collective-permute-start | bytes 589832 | tf_op jit(solution)/shard_map/ppermute | solution.py:31
  224.7 7.8 collective-permute-start.16
  232.5 682.0 %all-reduce.5.cloned.1.call-start = ((), (), s32[]{:S(2)}) async-start(), calls=%async_computation | async-start | bytes 1572864 | tf_op jit(solution)/shard_map/psum | solution.py:130
  233.7 256.4 %collective-permute-start.18 = (f32[2,384,64]{2,1,0:T(8,128)S(1)}, f32[2,384,64]{2,1,0:T(8,128)S(1)}, u32[]{:S(2)}, u32[]{:S(2)}) collective-permute-start(f32[2,384,64]{2,1,0:T(8,128)S(1)} %get-tuple-element.258), channel_id=1, source_target_pairs={{0,1},{1,2},{2,3},{3,4},{4,5},{5,6},{6,7},{8,9},{9,10},{10,11},{11... | collective-permute-start | bytes 589832 | tf_op jit(solution)/shard_map/ppermute | solution.py:22
  235.1 255.1 %collective-permute-start.19 = (f32[2,384,64]{2,1,0:T(8,128)S(1)}, f32[2,384,64]{2,1,0:T(8,128)}, u32[]{:S(2)}, u32[]{:S(2)}) collective-permute-start(f32[2,384,64]{2,1,0:T(8,128)S(1)} %get-tuple-element.259), channel_id=1, source_target_pairs={{1,0},{2,1},{3,2},{4,3},{5,4},{6,5},{7,6},{9,8},{10,9},{11,10},{12... | collective-permute-start | bytes 589832 | tf_op jit(solution)/shard_map/ppermute | solution.py:23
  531.4 10.8 %collective-permute-start.20 = (f32[2,384,64]{2,1,0:T(8,128)S(1)}, f32[2,384,64]{2,1,0:T(8,128)S(1)}, u32[]{:S(2)}, u32[]{:S(2)}) collective-permute-start(f32[2,384,64]{2,1,0:T(8,128)S(1)} %get-tuple-element.243), channel_id=1, source_target_pairs={{0,1},{1,2},{2,3},{3,4},{4,5},{5,6},{6,7},{8,9},{9,10},{10,11},{11... | collective-permute-start | bytes 589832 | tf_op jit(solution)/shard_map/ppermute | solution.py:31
  535.6 17.8 %collective-permute-start.21 = (f32[2,384,64]{2,1,0:T(8,128)S(1)}, f32[2,384,64]{2,1,0:T(8,128)S(1)}, u32[]{:S(2)}, u32[]{:S(2)}) collective-permute-start(f32[2,384,64]{2,1,0:T(8,128)S(1)} %get-tuple-element.242), channel_id=1, source_target_pairs={{1,0},{2,1},{3,2},{4,3},{5,4},{6,5},{7,6},{9,8},{10,9},{11,10},{12... | collective-permute-start | bytes 589832 | tf_op jit(solution)/shard_map/ppermute | solution.py:31
  555.1 7.0 collective-permute-start.22
  572.7 12.3 %collective-permute-start.26 = (f32[2,384,64]{2,1,0:T(8,128)S(1)}, f32[2,384,64]{2,1,0:T(8,128)S(1)}, u32[]{:S(2)}, u32[]{:S(2)}) collective-permute-start(f32[2,384,64]{2,1,0:T(8,128)S(1)} %get-tuple-element.254), channel_id=1, source_target_pairs={{0,1},{1,2},{2,3},{3,4},{4,5},{5,6},{6,7},{8,9},{9,10},{10,11},{11... | collective-permute-start | bytes 589832 | tf_op jit(solution)/shard_map/ppermute | solution.py:22
  575.9 19.9 %collective-permute-start.27 = (f32[2,384,64]{2,1,0:T(8,128)S(1)}, f32[2,384,64]{2,1,0:T(8,128)S(1)}, u32[]{:S(2)}, u32[]{:S(2)}) collective-permute-start(f32[2,384,64]{2,1,0:T(8,128)S(1)} %get-tuple-element.255), channel_id=1, source_target_pairs={{1,0},{2,1},{3,2},{4,3},{5,4},{6,5},{7,6},{9,8},{10,9},{11,10},{12... | collective-permute-start | bytes 589832 | tf_op jit(solution)/shard_map/ppermute | solution.py:23
  630.7 13.5 %collective-permute-start.28 = (f32[2,384,64]{2,1,0:T(8,128)S(1)}, f32[2,384,64]{2,1,0:T(8,128)S(1)}, u32[]{:S(2)}, u32[]{:S(2)}) collective-permute-start(f32[2,384,64]{2,1,0:T(8,128)S(1)} %get-tuple-element.241), channel_id=1, source_target_pairs={{0,1},{1,2},{2,3},{3,4},{4,5},{5,6},{6,7},{8,9},{9,10},{10,11},{11... | collective-permute-start | bytes 589832 | tf_op jit(solution)/shard_map/ppermute | solution.py:31
  635.0 20.6 %collective-permute-start.29 = (f32[2,384,64]{2,1,0:T(8,128)S(1)}, f32[2,384,64]{2,1,0:T(8,128)S(1)}, u32[]{:S(2)}, u32[]{:S(2)}) collective-permute-start(f32[2,384,64]{2,1,0:T(8,128)S(1)} %get-tuple-element.240), channel_id=1, source_target_pairs={{1,0},{2,1},{3,2},{4,3},{5,4},{6,5},{7,6},{9,8},{10,9},{11,10},{12... | collective-permute-start | bytes 589832 | tf_op jit(solution)/shard_map/ppermute | solution.py:31
  657.4 6.6 collective-permute-start.30
  (27 other events, 764.4 us)
Sparse Core Ops, SparseCore 0:
  232.6 255.3 all-reduce.6
  660.5 253.9 all-reduce.4
where the time goes:
time: 935 us; the launch traced here: 925 us
  waiting for transfers between devices  632 us (68%)
  matrix products  95.6 us (10%)
  starting transfers between devices  89.1 us (10%)
  local copies, waits for them, and re-layouts  66.5 us (7%)
  between operations  23.1 us (2%)
  other arithmetic  18 us (2%)
    psum x2, waiting for transfers between devices, per_device(): lax.psum((grad_sum, light_sum), ('stripe', 'tile'))  499 us
    ppermute x16, waiting for transfers between devices, from_behind(): lax.ppermute(value, axis, [(source, source + steps) for source in range(f...  73.4 us
    dot_general x32, matrix products, apply_right(): jnp.einsum('pkn,nm->pkm', batch, matrix, preferred_element_type=jnp.float32)  56.7 us
    ppermute x16, starting transfers between devices, from_behind(): lax.ppermute(value, axis, [(source, source + steps) for source in range(f...  45.5 us
    dot_general x32, matrix products, apply_left(): jnp.einsum('kn,pnm->pkm', matrix, batch, preferred_element_type=jnp.float32)  38.9 us
    ppermute x8, waiting for transfers between devices, padded(): after = lax.ppermute(first, axis, down)  36.3 us
    dynamic_update_slice x12, local copies, waits for them, and re-layouts, per_device(): lax.dynamic_update_slice(gradient, before + object_grad[pattern], where)  33.7 us
    ppermute x8, starting transfers between devices, padded(): before = lax.ppermute(last, axis, up)  28.4 us
  transfers between devices with their start and end apart: 34, of which 23 were waited for; matrix products, arithmetic and copies ran while one was open for 1% of the time, Pallas kernels for 0%

commit v1 on v0

--- a/solution.py
+++ b/solution.py
@@ -127,7 +127,7 @@
             own_grad = own_grad.at[:, :HALO, :].add(from_above)
             own_grad = own_grad.at[:, PW - HALO :, :].add(from_below)
             current = current - step_size * own_grad
-        total_grad, total_light = lax.psum((grad_sum, light_sum), ("stripe", "tile"))
+        total_grad, total_light = lax.psum(lax.psum((grad_sum, light_sum), "stripe"), "tile")
         probe_field = probe_field - 0.5 * total_grad / (total_light + 1.0)
     return (current, probe_field)
 

time: 935 us -> 1030 us (1.10)
  waiting for transfers between devices: 632 us -> 717 us
    psum x2 -> x4, waiting for transfers between devices: 499 us -> 564 us  [the longest x2 408 us: per_device(): lax.psum((grad_sum, light_sum), 'stripe')]
    ppermute x8, waiting for transfers between devices: 36.3 us -> 51.3 us  [padded(): after = lax.ppermute(first, axis, down)]
  transfers between devices with their start and end apart: 34 -> 36, of which waited for: 23 -> 27; matrix products, arithmetic and copies ran while one was open for 1% -> 2% of each run, Pallas kernels for 0% -> 0%
where the time goes in v1:
time: 1030 us; the launch traced here: 1010 us
  waiting for transfers between devices  717 us (70%)
  matrix products  95.6 us (9%)
  starting transfers between devices  92.6 us (9%)
  local copies, waits for them, and re-layouts  67.9 us (7%)
  between operations  23.1 us (2%)
  other arithmetic  18.1 us (2%)
    psum x2, waiting for transfers between devices, per_device(): lax.psum((grad_sum, light_sum), 'stripe')  408 us
    psum x2, waiting for transfers between devices, per_device(): lax.psum(lax.psum((grad_sum, light_sum), 'stripe'), 'tile')  156 us
    ppermute x16, waiting for transfers between devices, from_behind(): lax.ppermute(value, axis, [(source, source + steps) for source in range(f...  72.9 us
    dot_general x32, matrix products, apply_right(): jnp.einsum('pkn,nm->pkm', batch, matrix, preferred_element_type=jnp.float32)  56.8 us
    ppermute x8, waiting for transfers between devices, padded(): after = lax.ppermute(first, axis, down)  51.3 us
    ppermute x16, starting transfers between devices, from_behind(): lax.ppermute(value, axis, [(source, source + steps) for source in range(f...  45.7 us
    dot_general x32, matrix products, apply_left(): jnp.einsum('kn,pnm->pkm', matrix, batch, preferred_element_type=jnp.float32)  38.9 us
    dynamic_update_slice x12, local copies, waits for them, and re-layouts, per_device(): lax.dynamic_update_slice(gradient, before + object_grad[pattern], where)  33.7 us
  transfers between devices with their start and end apart: 36, of which 27 were waited for; matrix products, arithmetic and copies ran while one was open for 2% of the time, Pallas kernels for 0%

profile of v1, /device:TPU:2, one launch (start us, length us, event | category | flops | bytes accessed | tf_op | source)
XLA Modules:
  0.0 1014.9 jit_solution(14021291951107539343)
XLA Ops:
  27.7 7.7 collective-permute-done.2
  35.4 11.0 %collective-permute-done.3 = f32[2,384,64]{2,0,1:T(2,128)S(1)} collective-permute-done((f32[2,384,64]{2,0,1:T(2,128)S(1)}, f32[2,384,64]{2,0,1:T(2,128)S(1)}, u32[]{:S(2)}, u32[]{:S(2)}) %collective-permute-start.3) | collective-permute-done | bytes 196640 | tf_op jit(solution)/shard_map/ppermute | solution.py:23
  70.8 12.6 %subtract_bitcast_fusion.3 = (f32[3,1,256,256]{3,2,0,1:T(8,128)S(1)}, f32[3,1,256,256]{3,2,0,1:T(8,128)S(1)}) fusion(f32[3,256,256]{2,1,0:T(8,128)S(1)} %convolution_add_fusion.12, f32[256,256]{1,0:T(8,128)S(1)} %get-tuple-element.255, f32[256,256]{1,0:T(8,128)S(1)} %get-tuple-element.254, f32[3,256,256]{2,1,0:T(8,128)S(1)} %fusion.160, ...), kind=kOutput, calls=%fused_computation.134 | convolution fusion | flops 103088128 | bytes 4063232 | tf_op jit(solution)/shard_map/pkn,nm->pkm/dot_general | solution.py:50
  97.2 7.2 collective-permute-done.4
  105.5 9.0 collective-permute-done.5
  133.0 5.2 collective-permute-start.10
  139.4 7.8 collective-permute-done.10
  147.3 9.7 collective-permute-done.11
  191.8 5.3 collective-permute-start.12
  198.6 8.0 collective-permute-done.12
  207.7 8.1 collective-permute-done.13
  234.9 209.2 %all-reduce.11.cloned.1.call-done = (f32[2,256,256]{2,1,0:T(8,128)}, f32[256,256]{1,0:T(8,128)}) async-done(((f32[2,256,256]{2,1,0:T(8,128)}, f32[256,256]{1,0:T(8,128)}), (f32[2,256,256]{2,1,0:T(8,128)}, f32[256,256]{1,0:T(8,128)})) %all-reduce.11.cloned.1.call-update) | async-done | bytes 786448 | tf_op jit(solution)/shard_map/psum | solution.py:130
  449.7 7.4 collective-permute-done.18
  457.0 14.7 %collective-permute-done.19 = f32[2,384,64]{2,1,0:T(8,128)S(1)} collective-permute-done((f32[2,384,64]{2,1,0:T(8,128)S(1)}, f32[2,384,64]{2,1,0:T(8,128)S(1)}, u32[]{:S(2)}, u32[]{:S(2)}) %collective-permute-start.19) | collective-permute-done | bytes 196640 | tf_op jit(solution)/shard_map/ppermute | solution.py:23
  477.7 66.3 %all-reduce.15.cloned.1.call-done = (f32[2,256,256]{2,1,0:T(8,128)}, f32[256,256]{1,0:T(8,128)}) async-done(((f32[2,256,256]{2,1,0:T(8,128)}, f32[256,256]{1,0:T(8,128)}), (f32[2,256,256]{2,1,0:T(8,128)}, f32[256,256]{1,0:T(8,128)})) %all-reduce.15.cloned.1.call-update) | async-done | bytes 786448 | tf_op jit(solution)/shard_map/psum | solution.py:130
  590.2 9.1 collective-permute-done.21
  610.1 5.1 collective-permute-start.24
  623.8 6.4 collective-permute-done.26
  630.2 10.4 %collective-permute-done.27 = f32[2,384,64]{2,1,0:T(8,128)S(1)} collective-permute-done((f32[2,384,64]{2,1,0:T(8,128)S(1)}, f32[2,384,64]{2,1,0:T(8,128)S(1)}, u32[]{:S(2)}, u32[]{:S(2)}) %collective-permute-start.27) | collective-permute-done | bytes 196640 | tf_op jit(solution)/shard_map/ppermute | solution.py:23
  683.7 6.9 collective-permute-done.28
  691.7 13.2 %collective-permute-done.29 = f32[2,384,64]{2,1,0:T(8,128)S(1)} collective-permute-done((f32[2,384,64]{2,1,0:T(8,128)S(1)}, f32[2,384,64]{2,1,0:T(8,128)S(1)}, u32[]{:S(2)}, u32[]{:S(2)}) %collective-permute-start.29) | collective-permute-done | bytes 196640 | tf_op jit(solution)/shard_map/ppermute | solution.py:31
  706.7 199.1 %all-reduce.9.cloned.1.call-done = (f32[2,256,256]{2,1,0:T(8,128)}, f32[256,256]{1,0:T(8,128)}) async-done(((f32[2,256,256]{2,1,0:T(8,128)}, f32[256,256]{1,0:T(8,128)}), (f32[2,256,256]{2,1,0:T(8,128)}, f32[256,256]{1,0:T(8,128)})) %all-reduce.9.cloned.1.call-update) | async-done | bytes 786448 | tf_op jit(solution)/shard_map/psum | solution.py:130
  907.9 5.2 collective-permute-start.31
  915.8 89.3 %all-reduce.13.cloned.1.call-done = (f32[2,256,256]{2,1,0:T(8,128)}, f32[256,256]{1,0:T(8,128)}) async-done(((f32[2,256,256]{2,1,0:T(8,128)}, f32[256,256]{1,0:T(8,128)}), (f32[2,256,256]{2,1,0:T(8,128)}, f32[256,256]{1,0:T(8,128)})) %all-reduce.13.cloned.1.call-update) | async-done | bytes 786448 | tf_op jit(solution)/shard_map/psum | solution.py:130
  (270 shorter events, 257.8 us)
Async XLA Ops:
  7.2 436.9 %all-reduce.11.cloned.1.call-start = ((), (), s32[]{:S(2)}) async-start(), calls=%async_computation.1 | async-start | bytes 1572864 | tf_op jit(solution)/shard_map/psum | solution.py:130
  8.2 13.3 %collective-permute-start = (f32[2,64,128]{2,0,1:T(2,128)S(1)}, f32[2,64,128]{2,0,1:T(2,128)S(1)}, u32[]{:S(2)}, u32[]{:S(2)}) collective-permute-start(f32[2,64,128]{2,0,1:T(2,128)S(1)} %copy.230), channel_id=1, source_target_pairs={{0,8},{8,16},{16,24},{24,32},{32,40},{40,48},{48,56},{56,64},{64,7... | collective-permute-start | bytes 196616 | tf_op jit(solution)/shard_map/ppermute | solution.py:22
  10.2 11.6 %collective-permute-start.1 = (f32[2,64,128]{2,0,1:T(2,128)S(1)}, f32[2,64,128]{2,0,1:T(2,128)S(1)}, u32[]{:S(2)}, u32[]{:S(2)}) collective-permute-start(f32[2,64,128]{2,0,1:T(2,128)S(1)} %copy.231), channel_id=1, source_target_pairs={{8,0},{16,8},{24,16},{32,24},{40,32},{48,40},{56,48},{64,56},{72,6... | collective-permute-start | bytes 196616 | tf_op jit(solution)/shard_map/ppermute | solution.py:23
  22.3 13.1 %collective-permute-start.2 = (f32[2,384,64]{2,0,1:T(2,128)S(1)}, f32[2,384,64]{2,0,1:T(2,128)S(1)}, u32[]{:S(2)}, u32[]{:S(2)}) collective-permute-start(f32[2,384,64]{2,0,1:T(2,128)S(1)} %get-tuple-element.270), channel_id=1, source_target_pairs={{0,1},{1,2},{2,3},{3,4},{4,5},{5,6},{6,7},{8,9},{9,10},{10,11},{11... | collective-permute-start | bytes 589832 | tf_op jit(solution)/shard_map/ppermute | solution.py:22
  26.3 20.1 %collective-permute-start.3 = (f32[2,384,64]{2,0,1:T(2,128)S(1)}, f32[2,384,64]{2,0,1:T(2,128)S(1)}, u32[]{:S(2)}, u32[]{:S(2)}) collective-permute-start(f32[2,384,64]{2,0,1:T(2,128)S(1)} %get-tuple-element.271), channel_id=1, source_target_pairs={{1,0},{2,1},{3,2},{4,3},{5,4},{6,5},{7,6},{9,8},{10,9},{11,10},{12... | collective-permute-start | bytes 589832 | tf_op jit(solution)/shard_map/ppermute | solution.py:23
  91.2 13.2 %collective-permute-start.4 = (f32[2,384,64]{2,1,0:T(8,128)S(1)}, f32[2,384,64]{2,1,0:T(8,128)S(1)}, u32[]{:S(2)}, u32[]{:S(2)}) collective-permute-start(f32[2,384,64]{2,1,0:T(8,128)S(1)} %get-tuple-element.251), channel_id=1, source_target_pairs={{0,1},{1,2},{2,3},{3,4},{4,5},{5,6},{6,7},{8,9},{9,10},{10,11},{11... | collective-permute-start | bytes 589832 | tf_op jit(solution)/shard_map/ppermute | solution.py:31
  95.9 18.7 %collective-permute-start.5 = (f32[2,384,64]{2,1,0:T(8,128)S(1)}, f32[2,384,64]{2,1,0:T(8,128)S(1)}, u32[]{:S(2)}, u32[]{:S(2)}) collective-permute-start(f32[2,384,64]{2,1,0:T(8,128)S(1)} %get-tuple-element.250), channel_id=1, source_target_pairs={{1,0},{2,1},{3,2},{4,3},{5,4},{6,5},{7,6},{9,8},{10,9},{11,10},{12... | collective-permute-start | bytes 589832 | tf_op jit(solution)/shard_map/ppermute | solution.py:31
  133.0 14.3 %collective-permute-start.10 = (f32[2,384,64]{2,1,0:T(8,128)S(1)}, f32[2,384,64]{2,1,0:T(8,128)S(1)}, u32[]{:S(2)}, u32[]{:S(2)}) collective-permute-start(f32[2,384,64]{2,1,0:T(8,128)S(1)} %get-tuple-element.266), channel_id=1, source_target_pairs={{0,1},{1,2},{2,3},{3,4},{4,5},{5,6},{6,7},{8,9},{9,10},{10,11},{11... | collective-permute-start | bytes 589832 | tf_op jit(solution)/shard_map/ppermute | solution.py:22
  138.1 18.8 %collective-permute-start.11 = (f32[2,384,64]{2,1,0:T(8,128)S(1)}, f32[2,384,64]{2,1,0:T(8,128)S(1)}, u32[]{:S(2)}, u32[]{:S(2)}) collective-permute-start(f32[2,384,64]{2,1,0:T(8,128)S(1)} %get-tuple-element.267), channel_id=1, source_target_pairs={{1,0},{2,1},{3,2},{4,3},{5,4},{6,5},{7,6},{9,8},{10,9},{11,10},{12... | collective-permute-start | bytes 589832 | tf_op jit(solution)/shard_map/ppermute | solution.py:23
  191.8 14.8 %collective-permute-start.12 = (f32[2,384,64]{2,1,0:T(8,128)S(1)}, f32[2,384,64]{2,1,0:T(8,128)S(1)}, u32[]{:S(2)}, u32[]{:S(2)}) collective-permute-start(f32[2,384,64]{2,1,0:T(8,128)S(1)} %get-tuple-element.249), channel_id=1, source_target_pairs={{0,1},{1,2},{2,3},{3,4},{4,5},{5,6},{6,7},{8,9},{9,10},{10,11},{11... | collective-permute-start | bytes 589832 | tf_op jit(solution)/shard_map/ppermute | solution.py:31
  197.3 18.5 %collective-permute-start.13 = (f32[2,384,64]{2,1,0:T(8,128)S(1)}, f32[2,384,64]{2,1,0:T(8,128)S(1)}, u32[]{:S(2)}, u32[]{:S(2)}) collective-permute-start(f32[2,384,64]{2,1,0:T(8,128)S(1)} %get-tuple-element.248), channel_id=1, source_target_pairs={{1,0},{2,1},{3,2},{4,3},{5,4},{6,5},{7,6},{9,8},{10,9},{11,10},{12... | collective-permute-start | bytes 589832 | tf_op jit(solution)/shard_map/ppermute | solution.py:31
  220.4 323.6 %all-reduce.15.cloned.1.call-start = ((), (), s32[]{:S(2)}) async-start(), calls=%async_computation.3 | async-start | bytes 1572864 | tf_op jit(solution)/shard_map/psum | solution.py:130
  444.1 461.6 %all-reduce.9.cloned.1.call-start = ((), (), s32[]{:S(2)}) async-start(), calls=%async_computation | async-start | bytes 1572864 | tf_op jit(solution)/shard_map/psum | solution.py:130
  444.4 12.7 %collective-permute-start.18 = (f32[2,384,64]{2,1,0:T(8,128)S(1)}, f32[2,384,64]{2,1,0:T(8,128)S(1)}, u32[]{:S(2)}, u32[]{:S(2)}) collective-permute-start(f32[2,384,64]{2,1,0:T(8,128)S(1)} %get-tuple-element.262), channel_id=1, source_target_pairs={{0,1},{1,2},{2,3},{3,4},{4,5},{5,6},{6,7},{8,9},{9,10},{10,11},{11... | collective-permute-start | bytes 589832 | tf_op jit(solution)/shard_map/ppermute | solution.py:22
  448.4 23.3 %collective-permute-start.19 = (f32[2,384,64]{2,1,0:T(8,128)S(1)}, f32[2,384,64]{2,1,0:T(8,128)S(1)}, u32[]{:S(2)}, u32[]{:S(2)}) collective-permute-start(f32[2,384,64]{2,1,0:T(8,128)S(1)} %get-tuple-element.263), channel_id=1, source_target_pairs={{1,0},{2,1},{3,2},{4,3},{5,4},{6,5},{7,6},{9,8},{10,9},{11,10},{12... | collective-permute-start | bytes 589832 | tf_op jit(solution)/shard_map/ppermute | solution.py:23
  581.8 7.3 collective-permute-start.20
  584.0 15.3 %collective-permute-start.21 = (f32[2,384,64]{2,1,0:T(8,128)S(1)}, f32[2,384,64]{2,1,0:T(8,128)S(1)}, u32[]{:S(2)}, u32[]{:S(2)}) collective-permute-start(f32[2,384,64]{2,1,0:T(8,128)S(1)} %get-tuple-element.246), channel_id=1, source_target_pairs={{1,0},{2,1},{3,2},{4,3},{5,4},{6,5},{7,6},{9,8},{10,9},{11,10},{12... | collective-permute-start | bytes 589832 | tf_op jit(solution)/shard_map/ppermute | solution.py:31
  619.2 11.1 %collective-permute-start.26 = (f32[2,384,64]{2,1,0:T(8,128)S(1)}, f32[2,384,64]{2,1,0:T(8,128)S(1)}, u32[]{:S(2)}, u32[]{:S(2)}) collective-permute-start(f32[2,384,64]{2,1,0:T(8,128)S(1)} %get-tuple-element.258), channel_id=1, source_target_pairs={{0,1},{1,2},{2,3},{3,4},{4,5},{5,6},{6,7},{8,9},{9,10},{10,11},{11... | collective-permute-start | bytes 589832 | tf_op jit(solution)/shard_map/ppermute | solution.py:22
  622.5 18.1 %collective-permute-start.27 = (f32[2,384,64]{2,1,0:T(8,128)S(1)}, f32[2,384,64]{2,1,0:T(8,128)S(1)}, u32[]{:S(2)}, u32[]{:S(2)}) collective-permute-start(f32[2,384,64]{2,1,0:T(8,128)S(1)} %get-tuple-element.259), channel_id=1, source_target_pairs={{1,0},{2,1},{3,2},{4,3},{5,4},{6,5},{7,6},{9,8},{10,9},{11,10},{12... | collective-permute-start | bytes 589832 | tf_op jit(solution)/shard_map/ppermute | solution.py:23
  677.2 327.8 %all-reduce.13.cloned.1.call-start = ((), (), s32[]{:S(2)}) async-start(), calls=%async_computation.2 | async-start | bytes 1572864 | tf_op jit(solution)/shard_map/psum | solution.py:130
  677.4 13.2 %collective-permute-start.28 = (f32[2,384,64]{2,1,0:T(8,128)S(1)}, f32[2,384,64]{2,1,0:T(8,128)S(1)}, u32[]{:S(2)}, u32[]{:S(2)}) collective-permute-start(f32[2,384,64]{2,1,0:T(8,128)S(1)} %get-tuple-element.245), channel_id=1, source_target_pairs={{0,1},{1,2},{2,3},{3,4},{4,5},{5,6},{6,7},{8,9},{9,10},{10,11},{11... | collective-permute-start | bytes 589832 | tf_op jit(solution)/shard_map/ppermute | solution.py:31
  682.4 22.6 %collective-permute-start.29 = (f32[2,384,64]{2,1,0:T(8,128)S(1)}, f32[2,384,64]{2,1,0:T(8,128)S(1)}, u32[]{:S(2)}, u32[]{:S(2)}) collective-permute-start(f32[2,384,64]{2,1,0:T(8,128)S(1)} %get-tuple-element.244), channel_id=1, source_target_pairs={{1,0},{2,1},{3,2},{4,3},{5,4},{6,5},{7,6},{9,8},{10,9},{11,10},{12... | collective-permute-start | bytes 589832 | tf_op jit(solution)/shard_map/ppermute | solution.py:31
  905.8 7.3 collective-permute-start.30
  907.9 7.1 collective-permute-start.31
  (29 other events, 743.9 us)
Sparse Core Ops, SparseCore 0:
  220.5 223.5 all-reduce.10
  446.8 97.1 all-reduce.14
  677.3 228.3 all-reduce.8
  908.3 96.6 all-reduce.12
